TPU v7x, 32 devices: a whole 2x2x4 slice. The times are simulated.
32 devices in a mesh: ctx: 8 (over z, y), ch: 4 (over x, core).
Axes of the slice: x: 2, y: 2, z: 4, core: 2. Of those that a mesh axis runs over, the one named last changes fastest.
Arguments:
- query: bfloat16 [32768, 512], P('ctx', 'ch'), parts along dimension 1, may hold values from -6 to 6
- key_proj: bfloat16 [32768, 512], P('ctx', 'ch'), parts along dimension 1, may hold values from -6 to 6
- value: bfloat16 [32768, 512], P('ctx', 'ch'), parts along dimension 1, may hold values from -6 to 6
- short_taps: float32 [3, 3, 512], P(None, None, 'ch'), parts along dimension 2, may hold values from -3.5 to 3.5
- bias: float32 [512], P('ch'), parts along dimension 0, may hold values from -4 to 4
- long_filter: bfloat16 [32768, 512], P('ctx', 'ch'), parts along dimension 1, may hold values from -0.03125 to 0.03125
Outputs:
- gated: bfloat16 [32768, 512], P('ctx', 'ch'), parts along dimension 1
There are 4 independent parts, one for each index of `ch`. A program takes and returns all parts, laid end to end along the dimension named above; each array names one. Nothing has to cross between parts.
All inputs are finite; a program needn't handle non-finite values.
Results may differ from a plain program's by a relative error of at most 0.006.
Values may be sent and summed in bfloat16 or wider, within the bound.
A program may use at most 128 MiB of HBM per device.

v0:
```python
import math

import jax
import jax.numpy as jnp
from jax import lax
from jax.sharding import PartitionSpec as P

HIGH = lax.Precision.HIGHEST
TWO_PI = 2.0 * math.pi


def from_behind(block, axis, distance):
    devices = range(lax.axis_size(axis))
    route = [(i - distance, i) for i in devices if i - distance in devices]
    return lax.ppermute(block, axis, route)


def spin_table(count_out, count_in, period, factor):
    outer_index = jnp.arange(count_out, dtype=jnp.int32)[:, None]
    inner_index = jnp.arange(count_in, dtype=jnp.int32)[None, :]
    angle = TWO_PI / period * (outer_index * inner_index % period).astype(jnp.float32)
    return (factor * jnp.cos(angle), -factor * jnp.sin(angle))


def conj_table(period):
    cosine_part, sine_part = spin_table(period, period, period, 1.0)
    return (cosine_part, -sine_part)


def complex_dot(form, table_pair, value_pair):
    real_real = jnp.einsum(form, table_pair[0], value_pair[0], precision=HIGH)
    imag_imag = jnp.einsum(form, table_pair[1], value_pair[1], precision=HIGH)
    real_imag = jnp.einsum(form, table_pair[0], value_pair[1], precision=HIGH)
    imag_real = jnp.einsum(form, table_pair[1], value_pair[0], precision=HIGH)
    return (real_real - imag_imag, real_imag + imag_real)


def complex_scale(value_pair, factor_pair):
    first = value_pair[0] * factor_pair[0] - value_pair[1] * factor_pair[1]
    second = value_pair[0] * factor_pair[1] + value_pair[1] * factor_pair[0]
    return (first, second)


def featurize(stream, before, taps):
    length = stream.shape[0]
    count = taps.shape[0]
    extended = jnp.concatenate([before, stream], axis=0)
    total = jnp.zeros(stream.shape, jnp.float32)
    for offset in range(count):
        total = total + taps[offset] * extended[
            count - 1 - offset : count - 1 - offset + length
        ].astype(jnp.float32)
    return total


def filtered_lanes(lane_real, lane_imag, lane_freq, period):
    lanes, length, doubled = lane_real.shape
    width = doubled // 2
    inner = 128
    outer = length // inner
    positions = jnp.arange(length, dtype=jnp.int32)
    angle = TWO_PI / period * (lane_freq[:, None] * positions[None, :] % period).astype(jnp.float32)
    cosine = jnp.cos(angle)[:, :, None]
    sine = jnp.sin(angle)[:, :, None]
    turned = (lane_real * cosine + lane_imag * sine, lane_imag * cosine - lane_real * sine)
    grid = (
        turned[0].reshape(lanes, outer, inner, doubled),
        turned[1].reshape(lanes, outer, inner, doubled),
    )
    first = complex_dot("ea,labc->lebc", spin_table(outer, outer, outer, 1.0), grid)
    twist = spin_table(outer, inner, length, 1.0)
    first = complex_scale(first, (twist[0][None, :, :, None], twist[1][None, :, :, None]))
    spectrum = complex_dot("fb,lebc->elfc", spin_table(inner, inner, inner, 1.0), first)
    product = complex_scale(
        (spectrum[0][..., :width], spectrum[1][..., :width]),
        (spectrum[0][..., width:], spectrum[1][..., width:]),
    )
    backward = complex_dot("bf,elfc->lebc", conj_table(inner), product)
    backward = complex_scale(backward, (twist[0][None, :, :, None], -twist[1][None, :, :, None]))
    series = complex_dot("ae,lebc->labc", conj_table(outer), backward)
    series_real = series[0].reshape(lanes, length, width)
    series_imag = series[1].reshape(lanes, length, width)
    return (series_real * cosine - series_imag * sine, series_real * sine + series_imag * cosine)


def forward_direct(columns):
    parts = columns.shape[0]
    table = spin_table(2 * parts, parts, 2 * parts, 1.0)
    data = columns.astype(jnp.float32)
    part_real = jnp.einsum("kn,nsc->ksc", table[0], data, precision=HIGH)
    part_imag = jnp.einsum("kn,nsc->ksc", table[1], data, precision=HIGH)
    return (
        lax.all_to_all(part_real, "ctx", split_axis=0, concat_axis=1, tiled=True),
        lax.all_to_all(part_imag, "ctx", split_axis=0, concat_axis=1, tiled=True),
    )


def to_sequence(pieces, table_pair):
    rows_out = jnp.einsum("nk,ksc->nsc", table_pair[0], pieces[0], precision=HIGH)
    rows_out = rows_out + jnp.einsum("nk,ksc->nsc", table_pair[1], pieces[1], precision=HIGH)
    return lax.all_to_all(
        rows_out.astype(jnp.bfloat16), "ctx", split_axis=0, concat_axis=1, tiled=True
    )


def local(query, key_proj, value, short_taps, bias, long_filter):
    length, width = query.shape
    parts = lax.axis_size("ctx")
    member = lax.axis_index("ctx")
    period = 2 * length * parts
    keep = short_taps.shape[1] - 1
    edges = jnp.stack([query[length - keep :], key_proj[length - keep :], value[length - keep :]])
    before = from_behind(edges, "ctx", 1)
    query_feat = featurize(query, before[0], short_taps[0]).astype(jnp.bfloat16)
    query_wide = lax.optimization_barrier(query_feat).astype(jnp.float32)
    key_feat = featurize(key_proj, before[1], short_taps[1])
    value_feat = featurize(value, before[2], short_taps[2])
    mixed = (key_feat * value_feat).astype(jnp.bfloat16)
    joined = jnp.concatenate([mixed, long_filter], axis=1)
    lanes = forward_direct(
        lax.all_to_all(
            joined.reshape(1, length, 2 * width), "ctx", split_axis=1, concat_axis=0, tiled=True
        )
    )
    lane_freq = 2 * member + jnp.arange(2, dtype=jnp.int32)
    result_real, result_imag = filtered_lanes(lanes[0], lanes[1], lane_freq, period)
    table = spin_table(parts, 2 * parts, 2 * parts, 1.0 / period)
    rebuilt = to_sequence(
        (
            lax.all_to_all(result_real, "ctx", split_axis=1, concat_axis=0, tiled=True),
            lax.all_to_all(result_imag, "ctx", split_axis=1, concat_axis=0, tiled=True),
        ),
        table_pair=table,
    )
    convolved = rebuilt[0].astype(jnp.float32)
    return (query_wide * (convolved + bias * mixed.astype(jnp.float32))).astype(jnp.bfloat16)


def solution(mesh):
    in_specs = (
        P("ctx", "ch"),
        P("ctx", "ch"),
        P("ctx", "ch"),
        P(None, None, "ch"),
        P("ch"),
        P("ctx", "ch"),
    )
    out_specs = P("ctx", "ch")
    return jax.shard_map(local, mesh=mesh, in_specs=in_specs, out_specs=out_specs, check_vma=False)
```

profile of v0, /device:TPU:0, one launch (start us, length us, event | category | flops | bytes accessed | tf_op | source)
XLA Modules:
  0.0 962.0 jit_solution(8743161736265230253)
XLA Ops:
  1.4 4.9 collective-permute-start
  14.9 25.1 %copy.184 = bf16[1,4096,256]{2,0,1:T(2,128)(2,1)} copy(bf16[1,4096,256]{2,1,0:T(8,128)(2,1)S(1)} %maximum_bitcast_fusion) | data formatting | bytes 4194304 | tf_op jit(solution)/shard_map/reshape | solution.py:122
  40.5 21.6 %reduce = bf16[4096,256]{1,0:T(8,128)(2,1)S(1)} reduce(bf16[4096,1,256]{2,1,0:T(2,128)(2,1)} %bitcast.178, bf16[]{:T(256)} %broadcast.432), dimensions={1}, to_apply=%bitcast.171.reduce_sub_computation | reduce | bytes 4194306
  65.3 53.7 %all_to_all.93 = bf16[8,2,65536]{2,1,0:T(2,128)(2,1)S(1)} all-to-all(bf16[8,2,65536]{2,1,0:T(2,128)(2,1)} %reshape.181), channel_id=1, replica_groups=mesh['ctx'=8,'ch'=4] {'ctx'}, dimensions={0} | all-to-all | bytes 4194304 | tf_op jit(solution)/shard_map/all_to_all | solution.py:121
  130.0 8.1 copy.119
  138.1 5.2 all-to-all-start.2
  147.4 8.1 copy.116
  155.5 169.8 %all-to-all-done.2 = f32[16,512,256]{2,1,0:T(8,128)} async-done(((f32[16,512,256]{2,1,0:T(8,128)}), f32[16,512,256]{2,1,0:T(8,128)}, u32[]{:S(2)}, u32[]{:S(2)}) %all-to-all-start.2) | async-done | bytes 8388640 | tf_op jit(solution)/shard_map/all_to_all | solution.py:94
  325.3 5.4 all-to-all-start.1
  332.0 7.4 copy.120
  339.3 173.4 %all-to-all-done.1 = f32[16,512,256]{2,1,0:T(8,128)} async-done(((f32[16,512,256]{2,1,0:T(8,128)}), f32[16,512,256]{2,1,0:T(8,128)}, u32[]{:S(2)}, u32[]{:S(2)}) %all-to-all-start.1) | async-done | bytes 8388640 | tf_op jit(solution)/shard_map/all_to_all | solution.py:93
  521.4 13.1 %fusion.6 = f32[2,128,256,32]{2,3,1,0:T(8,128)} fusion(f32[2,32,128,256]{3,2,1,0:T(8,128)S(1)} %get-tuple-element.7), kind=kOutput, calls=%fused_computation.14 | convolution fusion | flops 805321728 | bytes 16777216 | tf_op jit(solution)/shard_map/ea,labc->lebc/dot_general | solution.py:34
  534.6 13.4 %fusion.8 = f32[2,128,256,32]{2,3,1,0:T(8,128)} fusion(f32[2,32,128,256]{3,2,1,0:T(8,128)S(1)} %get-tuple-element.7), kind=kOutput, calls=%fused_computation.16 | convolution fusion | flops 805320704 | bytes 16777216 | tf_op jit(solution)/shard_map/ea,labc->lebc/dot_general | solution.py:31
  548.0 13.1 %fusion.4 = f32[2,128,256,32]{2,3,1,0:T(8,128)} fusion(f32[2,32,128,256]{3,2,1,0:T(8,128)S(1)} %get-tuple-element.8), kind=kOutput, calls=%fused_computation.12 | convolution fusion | flops 805321728 | bytes 16777216 | tf_op jit(solution)/shard_map/ea,labc->lebc/dot_general | solution.py:32
  561.1 25.5 %fusion = (f32[2,32,128,256]{3,1,2,0:T(8,128)}, f32[2,32,128,256]{3,1,2,0:T(8,128)}) fusion(f32[32,128]{0,1:T(8,128)S(1)} %copy.126, f32[32,128]{0,1:T(8,128)S(1)} %copy.123, f32[2,128,256,32]{2,3,1,0:T(8,128)} %fusion.6, f32[2,128,256,32]{2,3,1,0:T(8,128)} %fusion.8, f32[2,128,256,32]{2,3,1,0:T(8,128)} %fusion.4, f32[2,32,128,256]{3,2,1,0:T(8,128)} %copy-done.1), kind=kOutput, calls=%fused_computation.2 | convolution fusion | flops 822097920 | bytes 50364416 | tf_op jit(solution)/shard_map/ea,labc->lebc/dot_general | solution.py:33
  586.5 10.1 %copy.128 = f32[2,32,128,256]{2,3,1,0:T(8,128)} copy(f32[2,32,128,256]{3,1,2,0:T(8,128)} %get-tuple-element.6) | data formatting | bytes 16777216 | tf_op jit(solution)/shard_map/add | solution.py:40
  596.7 11.5 %fusion.44 = f32[2,32,256,128]{3,2,1,0:T(8,128)} fusion(f32[2,32,128,256]{2,3,1,0:T(8,128)} %copy.128), kind=kOutput, calls=%fused_computation.77 | convolution fusion | flops 3221454848 | bytes 16777216 | tf_op jit(solution)/shard_map/fb,lebc->elfc/dot_general | solution.py:33
  608.2 10.0 %copy.127 = f32[2,32,128,256]{2,3,1,0:T(8,128)} copy(f32[2,32,128,256]{3,1,2,0:T(8,128)} %get-tuple-element.5) | data formatting | bytes 16777216 | tf_op jit(solution)/shard_map/sub | solution.py:39
  618.2 10.6 %fusion.46 = f32[2,32,256,128]{3,2,1,0:T(8,128)S(1)} fusion(f32[2,32,128,256]{2,3,1,0:T(8,128)} %copy.127), kind=kOutput, calls=%fused_computation.79 | convolution fusion | flops 3221454848 | bytes 16777216 | tf_op jit(solution)/shard_map/fb,lebc->elfc/dot_general | solution.py:31
  628.9 7.4 add_bitcast_fusion
  636.2 10.3 %subtract_bitcast_fusion = f32[32,2,128,256]{2,3,0,1:T(8,128)S(1)} fusion(f32[2,32,256,128]{3,2,1,0:T(8,128)S(1)} %fusion.46, f32[2,32,128,256]{2,3,1,0:T(8,128)} %copy.128), kind=kOutput, calls=%fused_computation.7 | convolution fusion | flops 3223568384 | bytes 25165824 | tf_op jit(solution)/shard_map/fb,lebc->elfc/dot_general | solution.py:32
  660.2 7.4 subtract_bitcast_fusion.2
  667.6 5.5 copy.136
  673.1 8.0 fusion.82
  681.1 5.5 copy.135
  686.6 6.1 fusion.84
  705.4 5.5 fusion.11
  710.9 16.1 %copy.141 = f32[2,4096,128]{2,0,1:T(2,128)} copy(f32[2,4096,128]{2,1,0:T(8,128)S(1)} %get-tuple-element.12) | data formatting | bytes 8388608 | tf_op jit(solution)/shard_map/sub | solution.py:83
  731.6 8.9 copy.144
  740.4 83.8 %all-to-all-done.3 = f32[2,4096,128]{2,0,1:T(2,128)} async-done(((f32[2,4096,128]{2,0,1:T(2,128)}), f32[2,4096,128]{2,0,1:T(2,128)}, u32[]{:S(2)}, u32[]{:S(2)}) %all-to-all-start.3) | async-done | bytes 4194336 | tf_op jit(solution)/shard_map/all_to_all | solution.py:130
  836.9 84.4 %all-to-all-done.4 = f32[2,4096,128]{2,0,1:T(2,128)} async-done(((f32[2,4096,128]{2,0,1:T(2,128)}), f32[2,4096,128]{2,0,1:T(2,128)}, u32[]{:S(2)}, u32[]{:S(2)}) %all-to-all-start.4) | async-done | bytes 4194336 | tf_op jit(solution)/shard_map/all_to_all | solution.py:131
  937.1 23.0 %all-to-all-done.5 = bf16[8,512,128]{2,1,0:T(8,128)(2,1)S(1)} async-done(((bf16[8,512,128]{2,1,0:T(8,128)(2,1)}), bf16[8,512,128]{2,1,0:T(8,128)(2,1)S(1)}, u32[]{:S(2)}, u32[]{:S(2)}) %all-to-all-start.5) | async-done | bytes 1048608 | tf_op jit(solution)/shard_map/all_to_all | solution.py:101
  (75 shorter events, 99.3 us)
Async XLA Ops:
  1.4 6.3 collective-permute-start
  13.1 26.9 %copy-start.6 = (bf16[4096,128]{1,0:T(8,128)(2,1)}, bf16[4096,128]{1,0:T(8,128)(2,1)S(1)}, u32[]{:S(2)}) copy-start(bf16[4096,128]{1,0:T(8,128)(2,1)S(1)} %multiply_convert_fusion) | copy-start | bytes 3145732
  138.1 187.2 %all-to-all-start.2 = ((f32[16,512,256]{2,1,0:T(8,128)}), f32[16,512,256]{2,1,0:T(8,128)}, u32[]{:S(2)}, u32[]{:S(2)}) async-start(f32[16,512,256]{2,1,0:T(8,128)} %copy.119), calls=%async_computation.2 | async-start | bytes 16777216 | tf_op jit(solution)/shard_map/all_to_all | solution.py:94
  325.3 187.4 %all-to-all-start.1 = ((f32[16,512,256]{2,1,0:T(8,128)}), f32[16,512,256]{2,1,0:T(8,128)}, u32[]{:S(2)}, u32[]{:S(2)}) async-start(f32[16,512,256]{2,1,0:T(8,128)} %copy.116), calls=%async_computation.1 | async-start | bytes 16777216 | tf_op jit(solution)/shard_map/all_to_all | solution.py:93
  512.7 4.6 slice-start
  512.8 5.9 slice-start.1
  521.4 26.5 %copy-start.1 = (f32[2,32,128,256]{3,2,1,0:T(8,128)}, f32[2,32,128,256]{3,2,1,0:T(8,128)S(1)}, u32[]{:S(2)}) copy-start(f32[2,32,128,256]{3,2,1,0:T(8,128)S(1)} %get-tuple-element.8) | copy-start | bytes 25165828
  618.2 10.6 %copy-start = (f32[2,32,128,256]{2,3,1,0:T(8,128)S(1)}, f32[2,32,128,256]{2,3,1,0:T(8,128)}, u32[]{:S(2)}) copy-start(f32[2,32,128,256]{2,3,1,0:T(8,128)} %copy.127) | copy-start | bytes 25165828
  618.2 10.6 %copy-start.2 = (f32[2,32,256,128]{3,2,1,0:T(8,128)S(1)}, f32[2,32,256,128]{3,2,1,0:T(8,128)}, u32[]{:S(2)}) copy-start(f32[2,32,256,128]{3,2,1,0:T(8,128)} %fusion.44) | copy-start | bytes 25165828
  686.6 6.2 copy-start.4
  686.6 6.2 copy-start.5
  696.5 2.4 copy-start.3
  727.0 97.2 %all-to-all-start.3 = ((f32[2,4096,128]{2,0,1:T(2,128)}), f32[2,4096,128]{2,0,1:T(2,128)}, u32[]{:S(2)}, u32[]{:S(2)}) async-start(f32[2,4096,128]{2,0,1:T(2,128)} %copy.141), calls=%async_computation.3 | async-start | bytes 8388608 | tf_op jit(solution)/shard_map/all_to_all | solution.py:130
  824.3 97.1 %all-to-all-start.4 = ((f32[2,4096,128]{2,0,1:T(2,128)}), f32[2,4096,128]{2,0,1:T(2,128)}, u32[]{:S(2)}, u32[]{:S(2)}) async-start(f32[2,4096,128]{2,0,1:T(2,128)} %copy.144), calls=%async_computation.4 | async-start | bytes 8388608 | tf_op jit(solution)/shard_map/all_to_all | solution.py:131
  927.1 7.0 copy-start.8
  927.1 7.0 copy-start.9
  927.1 7.0 copy-start.10
  927.1 7.0 copy-start.11
  929.3 30.8 %copy-start.7 = (bf16[4096,128]{1,0:T(8,128)(2,1)S(1)}, bf16[4096,128]{1,0:T(8,128)(2,1)}, u32[]{:S(2)}) copy-start(bf16[4096,128]{1,0:T(8,128)(2,1)} %copy-done.6) | copy-start | bytes 3145732
  929.3 30.7 %copy-start.12 = (f32[128]{0:T(128)S(1)}, f32[128]{0:T(128)}, u32[]{:S(2)}) copy-start(f32[128]{0:T(128)} %param.10) | copy-start | bytes 1540
  930.5 29.6 %all-to-all-start.5 = ((bf16[8,512,128]{2,1,0:T(8,128)(2,1)}), bf16[8,512,128]{2,1,0:T(8,128)(2,1)S(1)}, u32[]{:S(2)}, u32[]{:S(2)}) async-start(bf16[8,512,128]{2,1,0:T(8,128)(2,1)} %copy.147), calls=%async_computation.5 | async-start | bytes 2097152 | tf_op jit(solution)/shard_map/all_to_all | solution.py:101
where the time goes:
time: 969 us; the launch traced here: 962 us
  waiting for transfers between devices  534 us (55%)
  matrix products  158 us (16%)
  local copies, waits for them, and re-layouts  143 us (15%)
  blocking collectives  53.7 us (6%)
  other arithmetic  44.1 us (5%)
  starting transfers between devices  28.5 us (3%)
    all_to_all x1, waiting for transfers between devices, forward_direct(): lax.all_to_all(part_real, 'ctx', split_axis=0, concat_axis=1, tiled=True)  173 us
    all_to_all x1, waiting for transfers between devices, forward_direct(): lax.all_to_all(part_imag, 'ctx', split_axis=0, concat_axis=1, tiled=True)  170 us
    all_to_all x1, waiting for transfers between devices, local(): lax.all_to_all(result_imag, 'ctx', split_axis=1, concat_axis=0, tiled=True)  84.4 us
    all_to_all x1, waiting for transfers between devices, local(): lax.all_to_all(result_real, 'ctx', split_axis=1, concat_axis=0, tiled=True)  83.8 us
    all_to_all x1, blocking collectives, local(): lax.all_to_all(joined.reshape(1, length, 2 * width), 'ctx', split_axis=1,...  53.7 us
    dot_general x4, matrix products, complex_dot(): real_imag = jnp.einsum(form, table_pair[0], value_pair[1], precision=HIGH)  48.8 us
    dot_general x4, matrix products, complex_dot(): real_real = jnp.einsum(form, table_pair[0], value_pair[0], precision=HIGH)  33.9 us
    dot_general x4, matrix products, complex_dot(): imag_real = jnp.einsum(form, table_pair[1], value_pair[0], precision=HIGH)  31.7 us
  transfers between devices with their start and end apart: 6, of which 5 were waited for; matrix products, arithmetic and copies ran while one was open for 4% of the time, Pallas kernels for 0%

commit v1 on v0

v1 whole, which is shorter than its diff:
```python
import functools

import jax
import jax.numpy as jnp
import numpy as np
from jax import lax
from jax.experimental import pallas as pl
from jax.experimental.pallas import tpu as pltpu
from jax.sharding import PartitionSpec as P

BF = jnp.bfloat16
F32 = jnp.float32
ROWS = 32


def halves(table):
    table = np.asarray(table, np.float32)
    high = table.astype(jnp.bfloat16)
    return high, (table - high.astype(np.float32)).astype(jnp.bfloat16)


def make_tables(parts, length, width):
    group = width // parts
    fine = length // parts
    n = parts * length
    unit = np.arange(parts)
    v = np.arange(fine)
    place = parts * unit[:, None] + np.repeat(unit, group)[None, :]
    phase = place[None] * (unit[:, None, None] + 0.25) / parts**2
    coef = np.exp(-2j * np.pi * phase)
    coef = np.stack([coef.real, coef.imag]).astype(np.float32).reshape(2, parts * parts, width)
    short = np.kron(np.exp(-2j * np.pi * np.outer(unit, unit) / parts), np.eye(group))
    short = np.block([[short.real, short.imag], [-short.imag, short.real]])
    lane = np.exp(-2j * np.pi * np.outer(v, np.repeat(unit, group)) * parts / n)
    column = np.exp(-2j * np.pi * np.outer(v, unit + 0.25) / n)
    inner = np.exp(-2j * np.pi * (np.outer(v, v) % fine) / fine)
    c_h, c_l = halves(inner.real)
    s_h, s_l = halves(-inner.imag)

    def block(c, s):
        c, s = jnp.asarray(c), jnp.asarray(s)
        return jnp.concatenate(
            [jnp.concatenate([c, s], axis=1), jnp.concatenate([-s, c], axis=1)], axis=0
        )

    cr, ci = column.real.astype(np.float32).T[:, :, None], column.imag.astype(np.float32).T[:, :, None]
    lr, li = lane.real.astype(np.float32)[None], lane.imag.astype(np.float32)[None]
    spin = jnp.stack([cr * lr - ci * li, cr * li + ci * lr])
    short_h, short_l = halves(short)
    return coef, short_h, short_l, spin, block(c_h, s_h), block(c_l, s_l)


def dot(a, b):
    return jnp.dot(a, b, preferred_element_type=F32)


def split(value):
    high = value.astype(BF)
    return high, (value - high.astype(F32)).astype(BF)


def regroup(source, target, parts, fine, width):
    group = width // parts
    rows = min(fine, 128)
    lane = lax.broadcasted_iota(jnp.int32, (rows, width), 1) // group

    def step(i, carry):
        at = pl.ds(pl.multiple_of(i * rows, rows), rows)
        loaded = [source(w, at).astype(F32) for w in range(parts)]
        for d in range(parts):
            total = jnp.zeros((rows, width), F32)
            for w in range(parts):
                shift = ((w - d) % parts) * group
                moved = pltpu.roll(loaded[w], shift, 1) if shift else loaded[w]
                total = jnp.where(lane == w, moved, total)
            target(d, at, total.astype(BF))
        return carry

    lax.fori_loop(0, fine // rows, step, 0)


def pack_kernel(parts, fine, width, x_ref, o_ref):
    def load(w, at):
        return x_ref[w, at, :]

    def store(d, at, value):
        o_ref[d, at, :] = value

    regroup(load, store, parts, fine, width)


def forward(parts, fine, width, x_ref, coef, short_h, short_l, spin, big_h, big_l, z_h, z_l, y_h, y_l, finish):
    def first(i, carry):
        at = pl.ds(pl.multiple_of(i * ROWS, ROWS), ROWS)
        xs = [x_ref[j, at, :].astype(F32) for j in range(parts)]
        for a in range(parts):
            re = xs[0] * coef[0, a * parts][None]
            im = xs[0] * coef[1, a * parts][None]
            for j in range(1, parts):
                re = re + xs[j] * coef[0, a * parts + j][None]
                im = im + xs[j] * coef[1, a * parts + j][None]
            re_h, re_l = split(re)
            im_h, im_l = split(im)
            z_h[a, at, 0:width] = re_h
            z_l[a, at, 0:width] = re_l
            z_h[a, at, width:] = im_h
            z_l[a, at, width:] = im_l
        return carry

    lax.fori_loop(0, fine // ROWS, first, 0)

    def pair(p, carry):
        for e in range(2):
            a = 2 * p + e
            high = z_h[a]
            t = dot(high, short_h[...]) + dot(high, short_l[...]) + dot(z_l[a], short_h[...])
            re, im = t[:, :width], t[:, width:]
            sr, si = spin[0, a], spin[1, a]
            re_h, re_l = split(re * sr - im * si)
            im_h, im_l = split(re * si + im * sr)
            cols = slice(e * width, (e + 1) * width)
            y_h[0:fine, cols] = re_h
            y_l[0:fine, cols] = re_l
            y_h[fine:, cols] = im_h
            y_l[fine:, cols] = im_l
        high = y_h[...]
        out = dot(big_h[...], high) + dot(big_l[...], high) + dot(big_h[...], y_l[...])
        finish(p, out)
        return carry

    lax.fori_loop(0, parts // 2, pair, 0)


def filter_kernel(parts, fine, width, x_ref, coef, short_h, short_l, spin, big_h, big_l, o_ref, z_h, z_l, y_h, y_l):
    def finish(p, out):
        o_ref[p] = out

    forward(parts, fine, width, x_ref, coef, short_h, short_l, spin, big_h, big_l, z_h, z_l, y_h, y_l, finish)


def main_kernel(
    parts, fine, width, x_ref, h_ref, coef, short_h, short_l, spin, big_h, big_l, o_ref, z_h, z_l, y_h, y_l, u
):
    scale = float(1.0 / (parts * parts * fine))

    def finish(p, out):
        xr, xi = out[:fine], out[fine:]
        hr, hi = h_ref[p, 0:fine], h_ref[p, fine:]
        y_h[0:fine] = (xr * hr - xi * hi).astype(BF)
        y_h[fine:] = (-(xr * hi + xi * hr)).astype(BF)
        back = dot(big_h[...], y_h[...])
        for e in range(2):
            a = 2 * p + e
            cols = slice(e * width, (e + 1) * width)
            zr, zi = back[:fine, cols], -back[fine:, cols]
            sr, si = spin[0, a], spin[1, a]
            turned = jnp.concatenate([zr * sr + zi * si, zi * sr - zr * si], axis=1).astype(BF)
            u[a] = lax.dot_general(
                turned, short_h[...], (((1,), (1,)), ((), ())), preferred_element_type=F32
            )

    forward(parts, fine, width, x_ref, coef, short_h, short_l, spin, big_h, big_l, z_h, z_l, y_h, y_l, finish)

    def last(i, carry):
        at = pl.ds(pl.multiple_of(i * ROWS, ROWS), ROWS)
        for j in range(parts):
            total = jnp.zeros((ROWS, width), F32)
            for a in range(parts):
                total = total + u[a, at, 0:width] * coef[0, a * parts + j][None]
                total = total + u[a, at, width:] * coef[1, a * parts + j][None]
            o_ref[j, at, :] = (total * scale).astype(BF)
        return carry

    lax.fori_loop(0, fine // ROWS, last, 0)


def from_behind(block, axis, distance):
    devices = range(lax.axis_size(axis))
    route = [(i - distance, i) for i in devices if i - distance in devices]
    return lax.ppermute(block, axis, route)


def featurize(stream, before, taps):
    length = stream.shape[0]
    count = taps.shape[0]
    extended = jnp.concatenate([before, stream], axis=0)
    total = jnp.zeros(stream.shape, F32)
    for offset in range(count):
        total = total + taps[offset] * extended[count - 1 - offset : count - 1 - offset + length].astype(F32)
    return total


def local(query, key_proj, value, short_taps, bias, long_filter):
    length, width = query.shape
    parts = lax.axis_size("ctx")
    fine = length // parts
    keep = short_taps.shape[1] - 1
    tables = make_tables(parts, length, width)
    shape = (parts, fine, width)
    params = pltpu.CompilerParams(vmem_limit_bytes=56 * 1024 * 1024)
    scratch = [
        pltpu.VMEM((parts, fine, 2 * width), BF),
        pltpu.VMEM((parts, fine, 2 * width), BF),
        pltpu.VMEM((2 * fine, 2 * width), BF),
        pltpu.VMEM((2 * fine, 2 * width), BF),
    ]
    flops = 2 * 3 * parts * fine * (4 * width * width + 4 * fine * width)

    def call(body, out, scratch_shapes, work, *args):
        return pl.pallas_call(
            functools.partial(body, parts, fine, width),
            out_shape=out,
            scratch_shapes=scratch_shapes,
            compiler_params=params,
            cost_estimate=pl.CostEstimate(flops=work, bytes_accessed=8 << 20, transcendentals=0),
        )(*args)

    packed = jax.ShapeDtypeStruct(shape, BF)

    def pack(rows):
        return call(pack_kernel, packed, [], 1 << 20, rows.reshape(shape))

    def exchange(blocks):
        return lax.all_to_all(blocks, "ctx", split_axis=0, concat_axis=0, tiled=True)

    gathered_filter = exchange(pack(long_filter))
    edges = jnp.stack([query[length - keep :], key_proj[length - keep :], value[length - keep :]])
    before = from_behind(edges, "ctx", 1)
    query_feat = featurize(query, before[0], short_taps[0]).astype(BF)
    query_wide = lax.optimization_barrier(query_feat).astype(F32)
    mixed = (featurize(key_proj, before[1], short_taps[1]) * featurize(value, before[2], short_taps[2])).astype(BF)
    gathered = exchange(pack(mixed))
    spectrum = call(
        filter_kernel,
        jax.ShapeDtypeStruct((parts // 2, 2 * fine, 2 * width), F32),
        scratch,
        flops,
        gathered_filter,
        *tables,
    )
    rows = call(
        main_kernel,
        packed,
        scratch + [pltpu.VMEM((parts, fine, 2 * width), F32)],
        2 * flops,
        gathered,
        spectrum,
        *tables,
    )
    convolved = pack(exchange(rows)).reshape(length, width).astype(F32)
    return (query_wide * (convolved + bias * mixed.astype(F32))).astype(BF)


def solution(mesh):
    in_specs = (
        P("ctx", "ch"),
        P("ctx", "ch"),
        P("ctx", "ch"),
        P(None, None, "ch"),
        P("ch"),
        P("ctx", "ch"),
    )
    return jax.shard_map(local, mesh=mesh, in_specs=in_specs, out_specs=P("ctx", "ch"), check_vma=False)
```

time: 969 us -> 142 us (0.15)
  waiting for transfers between devices: 534 us -> 44.3 us
  matrix products: 158 us -> 0 us
  local copies, waits for them, and re-layouts: 143 us -> 2.7 us
  Pallas kernels: 0 us -> 62.5 us
  blocking collectives: 53.7 us -> 0 us
  other arithmetic: 44.1 us -> 8.09 us
    all_to_all x5 -> x3, waiting for transfers between devices: 534 us -> 42.1 us  [exchange(): lax.all_to_all(blocks, 'ctx', split_axis=0, concat_axis=0, tiled=True)]
    dot_general x20 -> x0, matrix products: 158 us -> none  [the longest x4 48.8 us: complex_dot(): real_imag = jnp.einsum(form, table_pair[0], value_pair[1], precision=HIGH)]
    pallas_call x0 -> x5, Pallas kernels: none -> 62.5 us  [call(): pl.pallas_call(functools.partial(body, parts, fine, width), out_shape=out...]
    all_to_all x1 -> x0, blocking collectives: 53.7 us -> none  [local(): lax.all_to_all(joined.reshape(1, length, 2 * width), 'ctx', split_axis=1,...]
    sub x4 -> x0, local copies, waits for them, and re-layouts: 34.3 us -> none  [the longest x1 16.1 us: filtered_lanes(): series_real * cosine - series_imag * sine]
    add x4 -> x0, local copies, waits for them, and re-layouts: 26.9 us -> none  [the longest x2 15.6 us: complex_scale(): second = value_pair[0] * factor_pair[1] + value_pair[1] * factor_pair[0]]
    reshape x1 -> x0, local copies, waits for them, and re-layouts: 25.1 us -> none  [local(): joined.reshape(1, length, 2 * width)]
    all_to_all x6 -> x0, local copies, waits for them, and re-layouts: 22.8 us -> none  [the longest x1 7.35 us: forward_direct(): lax.all_to_all(part_imag, 'ctx', split_axis=0, concat_axis=1, tiled=True)]
  transfers between devices with their start and end apart: 6 -> 4, of which waited for: 5 -> 4; matrix products, arithmetic and copies ran while one was open for 4% -> 4% of each run, Pallas kernels for 0% -> 16%
where the time goes in v1:
time: 142 us
  Pallas kernels  62.5 us (44%)
  waiting for transfers between devices  44.3 us (31%)
  starting transfers between devices  24.3 us (17%)
  other arithmetic  8.09 us (6%)
  local copies, waits for them, and re-layouts  2.7 us (2%)
    pallas_call x5, Pallas kernels, call(): pl.pallas_call(functools.partial(body, parts, fine, width), out_shape=out...  62.5 us
    all_to_all x3, waiting for transfers between devices, exchange(): lax.all_to_all(blocks, 'ctx', split_axis=0, concat_axis=0, tiled=True)  42.1 us
    all_to_all x3, starting transfers between devices, exchange(): lax.all_to_all(blocks, 'ctx', split_axis=0, concat_axis=0, tiled=True)  20.4 us
    ppermute x1, starting transfers between devices, from_behind(): return lax.ppermute(block, axis, route)  3.93 us
    convert_element_type x1, other arithmetic, local(): query_feat = featurize(query, before[0], short_taps[0]).astype(BF)  2.96 us
  transfers between devices with their start and end apart: 4, of which 4 were waited for; matrix products, arithmetic and copies ran while one was open for 4% of the time, Pallas kernels for 16%

profile of v1, /device:TPU:0, one launch (start us, length us, event | category | flops | bytes accessed | tf_op | source)
XLA Modules:
  0.0 142.0 jit_solution(16191737361705000764)
XLA Ops:
  0.0 0.0 copy-start.2
  0.0 0.0 copy-start.3
  0.0 0.0 copy-start.6
  0.0 4.5 %shard_map.146 = bf16[8,512,128]{2,1,0:T(8,128)(2,1)} custom-call(bf16[8,512,128]{2,1,0:T(8,128)(2,1)} %bitcast.36), custom_call_target="tpu_custom_call" | custom-call | flops 1048576 | bytes 8388608 | tf_op jit(solution)/shard_map/pallas_call | solution.py:210
  4.6 7.3 %all-to-all-start.1 = ((bf16[8,512,128]{2,1,0:T(8,128)(2,1)}), bf16[8,512,128]{2,1,0:T(8,128)(2,1)S(1)}, u32[]{:S(2)}, u32[]{:S(2)}) async-start(bf16[8,512,128]{2,1,0:T(8,128)(2,1)} %shard_map.146), calls=%async_computation.1 | async-start | bytes 2097152 | tf_op jit(solution)/shard_map/all_to_all | solution.py:224
  11.8 0.7 slice_bitcast_fusion.12
  12.5 0.0 copy-done.2
  12.5 0.0 copy-done.3
  12.6 3.9 %collective-permute-start = (bf16[3,2,128]{2,1,0:T(2,128)(2,1)S(1)}, bf16[3,2,128]{2,1,0:T(2,128)(2,1)S(1)}, u32[]{:S(2)}, u32[]{:S(2)}) collective-permute-start(bf16[3,2,128]{2,1,0:T(2,128)(2,1)S(1)} %pad_maximum_fusion.3), channel_id=1, source_target_pairs={{0,4},{4,8},{8,12},{12,16},{16,20},{20,24},{24,28},{1,5},{5,9},{9,... | collective-permute-start | bytes 4616 | tf_op jit(solution)/shard_map/ppermute | solution.py:180
  16.5 0.0 copy-done.6
  16.5 2.3 %collective-permute-done = bf16[3,2,128]{2,1,0:T(2,128)(2,1)S(1)} collective-permute-done((bf16[3,2,128]{2,1,0:T(2,128)(2,1)S(1)}, bf16[3,2,128]{2,1,0:T(2,128)(2,1)S(1)}, u32[]{:S(2)}, u32[]{:S(2)}) %collective-permute-start) | collective-permute-done | bytes 1568 | tf_op jit(solution)/shard_map/ppermute | solution.py:180
  18.8 2.4 %multiply_convert_fusion = bf16[4096,128]{1,0:T(8,128)(2,1)} fusion(bf16[4096,128]{1,0:T(8,128)(2,1)S(1)} %copy-done.2, bf16[4096,128]{1,0:T(8,128)(2,1)S(1)} %copy-done.3, bf16[2,128]{1,0:T(2,128)(2,1)S(1)} %get-tuple-element.15, bf16[2,128]{1,0:T(2,128)(2,1)S(1)} %get-tuple-element.16, f32[128]{0:T(128)S(1)} %get-tuple-element.12, ...), kind=kLoop, calls=%fused_computation.3 | loop fusion | flops 15728640 | bytes 3149824 | tf_op jit(solution)/shard_map/convert_element_type | solution.py:231
  21.2 4.4 %shard_map.145 = bf16[8,512,128]{2,1,0:T(8,128)(2,1)} custom-call(bf16[8,512,128]{2,1,0:T(8,128)(2,1)} %bitcast.35), custom_call_target="tpu_custom_call" | custom-call | flops 1048576 | bytes 8388608 | tf_op jit(solution)/shard_map/pallas_call | solution.py:210
  25.6 12.0 %all-to-all-done.1.x_ref = bf16[8,512,128]{2,1,0:T(8,128)(2,1)S(1)} async-done(((bf16[8,512,128]{2,1,0:T(8,128)(2,1)}), bf16[8,512,128]{2,1,0:T(8,128)(2,1)S(1)}, u32[]{:S(2)}, u32[]{:S(2)}) %all-to-all-start.1) | async-done | bytes 1048608 | tf_op jit(solution)/shard_map/all_to_all | solution.py:224
  37.6 0.0 copy-start.4
  37.6 9.6 %all-to-all-start = ((bf16[8,512,128]{2,1,0:T(8,128)(2,1)}), bf16[8,512,128]{2,1,0:T(8,128)(2,1)S(1)}, u32[]{:S(2)}, u32[]{:S(2)}) async-start(bf16[8,512,128]{2,1,0:T(8,128)(2,1)} %shard_map.145), calls=%async_computation | async-start | bytes 2097152 | tf_op jit(solution)/shard_map/all_to_all | solution.py:224
  47.2 0.0 copy-done.4
  47.2 18.5 %shard_map.147.h_ref = f32[4,1024,256]{2,1,0:T(8,128)} custom-call(bf16[8,512,128]{2,1,0:T(8,128)(2,1)} %copy-done.4, f32[2,64,128]{2,1,0:T(8,128)} %constant.24.clone.coef, bf16[256,256]{1,0:T(8,128)(2,1)} %constant.25.clone.short_h, bf16[256,256]{1,0:T(8,128)(2,1)} %constant.26.clone.short_l, f32[2,8,512,128]{3,2,1,0:T(8,128)} %constant.29.spin, ...), custom_call_target="tpu_custom_call" | custom-call | flops 8053063680 | bytes 8388608 | tf_op jit(solution)/shard_map/pallas_call | solution.py:210
  65.7 7.2 %all-to-all-done.x_ref = bf16[8,512,128]{2,1,0:T(8,128)(2,1)S(1)} async-done(((bf16[8,512,128]{2,1,0:T(8,128)(2,1)}), bf16[8,512,128]{2,1,0:T(8,128)(2,1)S(1)}, u32[]{:S(2)}, u32[]{:S(2)}) %all-to-all-start) | async-done | bytes 1048608 | tf_op jit(solution)/shard_map/all_to_all | solution.py:224
  72.9 0.0 copy-start.5
  72.9 1.0 copy-done.5
  73.9 30.6 %shard_map.148 = bf16[8,512,128]{2,1,0:T(8,128)(2,1)} custom-call(bf16[8,512,128]{2,1,0:T(8,128)(2,1)} %copy-done.5, f32[4,1024,256]{2,1,0:T(8,128)} %shard_map.147.h_ref, f32[2,64,128]{2,1,0:T(8,128)} %constant.24.clone.coef, bf16[256,256]{1,0:T(8,128)(2,1)} %constant.25.clone.short_h, bf16[256,256]{1,0:T(8,128)(2,1)} %constant.26.clone.short_l, ...), custom_call_target="tpu_custom_call" | custom-call | flops 16106127360 | bytes 8388608 | tf_op jit(solution)/shard_map/pallas_call | solution.py:210
  104.5 3.6 %all-to-all-start.2 = ((bf16[8,512,128]{2,1,0:T(8,128)(2,1)}), bf16[8,512,128]{2,1,0:T(8,128)(2,1)S(1)}, u32[]{:S(2)}, u32[]{:S(2)}) async-start(bf16[8,512,128]{2,1,0:T(8,128)(2,1)} %shard_map.148), calls=%async_computation.2 | async-start | bytes 2097152 | tf_op jit(solution)/shard_map/all_to_all | solution.py:224
  108.0 0.0 copy-start
  108.0 0.0 copy-start.7
  108.0 3.0 %add_convert_fusion = bf16[4096,128]{1,0:T(8,128)(2,1)S(1)} fusion(bf16[4096,128]{1,0:T(8,128)(2,1)} %param.15, bf16[2,128]{1,0:T(2,128)(2,1)S(1)} %get-tuple-element.14, f32[128]{0:T(128)S(1)} %get-tuple-element.10, f32[128]{0:T(128)S(1)} %get-tuple-element.11, f32[128]{0:T(128)S(1)} %get-tuple-element.5), kind=kLoop, calls=%fused_computation.4 | loop fusion | flops 7864320 | bytes 2099200 | tf_op jit(solution)/shard_map/convert_element_type | solution.py:229
  111.0 22.9 %all-to-all-done.2.x_ref = bf16[8,512,128]{2,1,0:T(8,128)(2,1)S(1)} async-done(((bf16[8,512,128]{2,1,0:T(8,128)(2,1)}), bf16[8,512,128]{2,1,0:T(8,128)(2,1)S(1)}, u32[]{:S(2)}, u32[]{:S(2)}) %all-to-all-start.2) | async-done | bytes 1048608 | tf_op jit(solution)/shard_map/all_to_all | solution.py:224
  134.0 1.0 copy-done.1
  134.9 4.4 %shard_map.149 = bf16[8,512,128]{2,1,0:T(8,128)(2,1)} custom-call(bf16[8,512,128]{2,1,0:T(8,128)(2,1)} %copy-done.1), custom_call_target="tpu_custom_call" | custom-call | flops 1048576 | bytes 8388608 | tf_op jit(solution)/shard_map/pallas_call | solution.py:210
  139.4 0.0 copy-done
  139.4 0.0 copy-done.7
  139.4 2.7 %fusion.1 = bf16[4096,128]{1,0:T(8,128)(2,1)} fusion(bf16[4096,128]{1,0:T(8,128)(2,1)S(1)} %copy-done, bf16[4096,128]{1,0:T(8,128)(2,1)S(1)} %add_convert_fusion, bf16[8,512,128]{2,1,0:T(8,128)(2,1)} %shard_map.149, f32[128]{0:T(128)S(1)} %copy-done.7), kind=kLoop, calls=%fused_computation.2 | loop fusion | flops 3670016 | bytes 4194816 | tf_op jit(solution)/shard_map/convert_element_type | solution.py:251
  (5 shorter events, 0.0 us)
Async XLA Ops:
  0.0 12.5 %copy-start.2 = (bf16[4096,128]{1,0:T(8,128)(2,1)S(1)}, bf16[4096,128]{1,0:T(8,128)(2,1)}, u32[]{:S(2)}) copy-start(bf16[4096,128]{1,0:T(8,128)(2,1)} %param.17) | copy-start | bytes 3145732
  0.0 12.5 %copy-start.3 = (bf16[4096,128]{1,0:T(8,128)(2,1)S(1)}, bf16[4096,128]{1,0:T(8,128)(2,1)}, u32[]{:S(2)}) copy-start(bf16[4096,128]{1,0:T(8,128)(2,1)} %param.16) | copy-start | bytes 3145732
  0.0 16.5 %copy-start.6 = (f32[3,3,128]{2,1,0:T(4,128)S(1)}, f32[3,3,128]{2,1,0:T(4,128)}, u32[]{:S(2)}) copy-start(f32[3,3,128]{2,1,0:T(4,128)} %param.18) | copy-start | bytes 13828
  4.6 33.1 %all-to-all-start.1 = ((bf16[8,512,128]{2,1,0:T(8,128)(2,1)}), bf16[8,512,128]{2,1,0:T(8,128)(2,1)S(1)}, u32[]{:S(2)}, u32[]{:S(2)}) async-start(bf16[8,512,128]{2,1,0:T(8,128)(2,1)} %shard_map.146), calls=%async_computation.1 | async-start | bytes 2097152 | tf_op jit(solution)/shard_map/all_to_all | solution.py:224
  12.6 6.2 %collective-permute-start = (bf16[3,2,128]{2,1,0:T(2,128)(2,1)S(1)}, bf16[3,2,128]{2,1,0:T(2,128)(2,1)S(1)}, u32[]{:S(2)}, u32[]{:S(2)}) collective-permute-start(bf16[3,2,128]{2,1,0:T(2,128)(2,1)S(1)} %pad_maximum_fusion.3), channel_id=1, source_target_pairs={{0,4},{4,8},{8,12},{12,16},{16,20},{20,24},{24,28},{1,5},{5,9},{9,... | collective-permute-start | bytes 4616 | tf_op jit(solution)/shard_map/ppermute | solution.py:180
  37.6 9.6 %copy-start.4 = (bf16[8,512,128]{2,1,0:T(8,128)(2,1)}, bf16[8,512,128]{2,1,0:T(8,128)(2,1)S(1)}, u32[]{:S(2)}) copy-start(bf16[8,512,128]{2,1,0:T(8,128)(2,1)S(1)} %all-to-all-done.1.x_ref) | copy-start | bytes 3145732
  37.6 35.3 %all-to-all-start = ((bf16[8,512,128]{2,1,0:T(8,128)(2,1)}), bf16[8,512,128]{2,1,0:T(8,128)(2,1)S(1)}, u32[]{:S(2)}, u32[]{:S(2)}) async-start(bf16[8,512,128]{2,1,0:T(8,128)(2,1)} %shard_map.145), calls=%async_computation | async-start | bytes 2097152 | tf_op jit(solution)/shard_map/all_to_all | solution.py:224
  72.9 1.0 copy-start.5
  104.5 29.5 %all-to-all-start.2 = ((bf16[8,512,128]{2,1,0:T(8,128)(2,1)}), bf16[8,512,128]{2,1,0:T(8,128)(2,1)S(1)}, u32[]{:S(2)}, u32[]{:S(2)}) async-start(bf16[8,512,128]{2,1,0:T(8,128)(2,1)} %shard_map.148), calls=%async_computation.2 | async-start | bytes 2097152 | tf_op jit(solution)/shard_map/all_to_all | solution.py:224
  108.0 31.3 %copy-start = (bf16[4096,128]{1,0:T(8,128)(2,1)S(1)}, bf16[4096,128]{1,0:T(8,128)(2,1)}, u32[]{:S(2)}) copy-start(bf16[4096,128]{1,0:T(8,128)(2,1)} %multiply_convert_fusion) | copy-start | bytes 3145732
  108.0 31.3 %copy-start.7 = (f32[128]{0:T(128)S(1)}, f32[128]{0:T(128)}, u32[]{:S(2)}) copy-start(f32[128]{0:T(128)} %param.19) | copy-start | bytes 1540
  134.0 1.0 copy-start.1

commit v2 on v0

v2 whole, which is shorter than its diff:
```python
import functools

import jax
import jax.numpy as jnp
import numpy as np
from jax import lax
from jax.experimental import pallas as pl
from jax.experimental.pallas import tpu as pltpu
from jax.sharding import PartitionSpec as P

BF = jnp.bfloat16
F32 = jnp.float32
ROWS = 32
CHUNKS = 2
MESH = pl.DeviceIdType.MESH


def halves(table):
    table = np.asarray(table, np.float32)
    high = table.astype(jnp.bfloat16)
    return high, (table - high.astype(np.float32)).astype(jnp.bfloat16)


def make_tables(parts, fold, length, width):
    group = width // fold
    fine = length // fold
    n = parts * length
    unit = np.arange(parts)
    block = np.arange(fold)
    v = np.arange(fine)
    place = fold * unit[:, None] + np.repeat(block, group)[None, :]
    phase = place[None] * (unit[:, None, None] + 0.25) / (parts * fold)
    coef = np.exp(-2j * np.pi * phase)
    coef = np.stack([coef.real, coef.imag]).astype(np.float32).reshape(2, parts * parts, width)
    short = np.kron(np.exp(-2j * np.pi * np.outer(block, block) / fold), np.eye(group))
    short = np.block([[short.real, short.imag], [-short.imag, short.real]])
    lane = np.exp(-2j * np.pi * np.outer(v, np.repeat(block, group)) * parts / n)
    column = np.exp(-2j * np.pi * np.outer(v, unit + 0.25) / n)
    inner = np.exp(-2j * np.pi * (np.outer(v, v) % fine) / fine)
    big = np.block([[inner.real, -inner.imag], [inner.imag, inner.real]])
    spin = column.T[:, :, None] * lane[None]
    spin = np.stack([spin.real, spin.imag]).astype(np.float32)
    return (coef, *halves(short), spin, *halves(big))


def dot(a, b):
    return jnp.dot(a, b, preferred_element_type=F32)


def split(value):
    high = value.astype(BF)
    return high, (value - high.astype(F32)).astype(BF)


def regroup(xs, fold, width):
    group = width // fold
    lane = lax.broadcasted_iota(jnp.int32, xs[0].shape, 1) // group
    bit = 1
    while bit < fold:
        high = (lane // bit) % 2 == 1
        out = list(xs)
        for i in range(fold):
            if i & bit == 0:
                low_x, high_x = xs[i], xs[i + bit]
                out[i] = jnp.where(high, pltpu.roll(high_x, bit * group, 1), low_x)
                out[i + bit] = jnp.where(high, high_x, pltpu.roll(low_x, width - bit * group, 1))
        xs = out
        bit *= 2
    return xs


def body(
    parts, fold, fine, width,
    q_ref, k_ref, v_ref, taps, bias, f_ref, coef, short_h, short_l, spin, big_h, big_l, o_ref,
    halo, mixed, q_feat, out_f, out_m, out_y, in_f, in_m, in_y,
    z_h, z_l, y_h, y_l, spectrum, u, send, recv, own, halo_send, halo_recv,
):
    me = lax.axis_index("ctx")
    chunks = fold // parts
    length = fold * fine
    scale = float(1.0 / (parts * length))
    count = taps.shape[1]
    streams = (q_ref, k_ref, v_ref)

    barrier = pltpu.get_barrier_semaphore()

    def greet(k, carry):
        pl.semaphore_signal(barrier, inc=1, device_id={"ctx": lax.rem(me + k, parts)}, device_id_type=MESH)
        return carry

    lax.fori_loop(1, parts, greet, 0)

    outs = (out_f, out_m, out_y)
    ins = (in_f, in_m, in_y)

    def remote(kind, g, k):
        there = lax.rem(me + k, parts)
        return pltpu.make_async_remote_copy(
            src_ref=outs[kind].at[g, there],
            dst_ref=ins[kind].at[g, me],
            send_sem=send.at[kind, g, there],
            recv_sem=recv.at[kind, g, me],
            device_id={"ctx": there},
            device_id_type=MESH,
        )

    def arrival(kind, g, k):
        there = lax.rem(me + k, parts)
        return pltpu.make_async_remote_copy(
            src_ref=outs[kind].at[g, there],
            dst_ref=ins[kind].at[g, there],
            send_sem=send.at[kind, g, there],
            recv_sem=recv.at[kind, g, there],
            device_id={"ctx": there},
            device_id_type=MESH,
        )

    def local_copy(kind, g):
        return pltpu.make_async_copy(outs[kind].at[g, me], ins[kind].at[g, me], own.at[kind, g])

    def start(kind, g):
        def go(k, carry):
            remote(kind, g, k).start()
            return carry

        lax.fori_loop(1, parts, go, 0)
        local_copy(kind, g).start()

    def wait(kind, g):
        def go(k, carry):
            arrival(kind, g, k).wait_recv()
            return carry

        lax.fori_loop(1, parts, go, 0)
        local_copy(kind, g).wait()

    def drain(kind, g):
        def go(k, carry):
            remote(kind, g, k).wait_send()
            return carry

        lax.fori_loop(1, parts, go, 0)

    def halo_copy(s):
        return pltpu.make_async_remote_copy(
            src_ref=streams[s].at[pl.ds(length - 16, 16)],
            dst_ref=halo.at[s],
            send_sem=halo_send.at[s],
            recv_sem=halo_recv.at[s],
            device_id={"ctx": lax.rem(me + 1, parts)},
            device_id_type=MESH,
        )

    tile = min(fine, max(16, 512 // fold))

    def pack(x_ref, target):
        def step(i, carry):
            xs = [
                x_ref[pl.ds(pl.multiple_of(w * fine + i * tile, tile), tile), :].astype(F32)
                for w in range(fold)
            ]
            moved = regroup(xs, fold, width)
            at = pl.ds(pl.multiple_of(i * tile, tile), tile)
            for e in range(fold):
                target[e % chunks, e // chunks, at, :] = moved[e].astype(BF)
            return carry

        lax.fori_loop(0, fine // tile, step, 0)

    pack(f_ref, out_f)
    pl.semaphore_wait(barrier, parts - 1)
    for s in range(3):
        halo_copy(s).start()
    for g in range(chunks):
        start(0, g)

    for s in range(3):
        halo_copy(s).wait_recv()
    inside = jnp.where(me == 0, 0.0, 1.0).astype(F32)
    rows = min(length, 64)

    def shifted(x_ref, s, at, tail):
        now = x_ref[at, :].astype(F32)
        extended = jnp.concatenate([tail, now], axis=0)
        total = taps[s, 0][None] * now
        for j in range(1, count):
            total = total + taps[s, j][None] * pltpu.roll(extended, j, 0)[8:]
        return total, now[rows - 8 :]

    tails = [halo[s].astype(F32)[8:] * inside for s in range(3)]

    def features(i, carry):
        at = pl.ds(pl.multiple_of(i * rows, rows), rows)
        key, key_tail = shifted(k_ref, 1, at, carry[0])
        val, val_tail = shifted(v_ref, 2, at, carry[1])
        mixed[at, :] = (key * val).astype(BF)
        return key_tail, val_tail

    lax.fori_loop(0, length // rows, features, (tails[1], tails[2]))
    pack(mixed, out_m)
    for g in range(chunks):
        start(1, g)

    def q_features(i, carry):
        at = pl.ds(pl.multiple_of(i * rows, rows), rows)
        total, tail = shifted(q_ref, 0, at, carry)
        q_feat[at, :] = total.astype(BF)
        return tail

    lax.fori_loop(0, length // rows, q_features, tails[0])

    def forward(x_ref, g, finish):
        def first(i, carry):
            at = pl.ds(pl.multiple_of(i * step_rows, step_rows), step_rows)
            xs = [x_ref[g, j, at, :].astype(F32) for j in range(parts)]
            for a in range(parts):
                re = xs[0] * coef[0, a * parts][None]
                im = xs[0] * coef[1, a * parts][None]
                for j in range(1, parts):
                    re = re + xs[j] * coef[0, a * parts + j][None]
                    im = im + xs[j] * coef[1, a * parts + j][None]
                re_h, re_l = split(re)
                im_h, im_l = split(im)
                z_h[a, at, 0:width] = re_h
                z_l[a, at, 0:width] = re_l
                z_h[a, at, width:] = im_h
                z_l[a, at, width:] = im_l
            return carry

        step_rows = min(fine, ROWS)
        lax.fori_loop(0, fine // step_rows, first, 0)

        def pair(p, carry):
            for e in range(2):
                a = 2 * p + e
                high = z_h[a]
                t = dot(high, short_h[...]) + dot(high, short_l[...]) + dot(z_l[a], short_h[...])
                re, im = t[:, :width], t[:, width:]
                sr, si = spin[0, a], spin[1, a]
                re_h, re_l = split(re * sr - im * si)
                im_h, im_l = split(re * si + im * sr)
                cols = slice(e * width, (e + 1) * width)
                y_h[0:fine, cols] = re_h
                y_l[0:fine, cols] = re_l
                y_h[fine:, cols] = im_h
                y_l[fine:, cols] = im_l
            high = y_h[...]
            out = dot(big_h[...], high) + dot(big_l[...], high) + dot(big_h[...], y_l[...])
            finish(p, out)
            return carry

        lax.fori_loop(0, parts // 2, pair, 0)

    for g in range(chunks):
        wait(0, g)

        def keep(p, out):
            spectrum[g, p] = out

        forward(in_f, g, keep)

    for g in range(chunks):
        wait(1, g)

        def finish(p, out):
            xr, xi = out[:fine], out[fine:]
            hr, hi = spectrum[g, p, 0:fine], spectrum[g, p, fine:]
            y_h[0:fine] = (xr * hr - xi * hi).astype(BF)
            y_h[fine:] = (-(xr * hi + xi * hr)).astype(BF)
            back = dot(big_h[...], y_h[...])
            for e in range(2):
                a = 2 * p + e
                cols = slice(e * width, (e + 1) * width)
                zr, zi = back[:fine, cols], -back[fine:, cols]
                sr, si = spin[0, a], spin[1, a]
                turned = jnp.concatenate([zr * sr + zi * si, zi * sr - zr * si], axis=1).astype(BF)
                u[a] = lax.dot_general(
                    turned, short_h[...], (((1,), (1,)), ((), ())), preferred_element_type=F32
                )

        forward(in_m, g, finish)
        step_rows = min(fine, ROWS)

        def last(i, carry):
            at = pl.ds(pl.multiple_of(i * step_rows, step_rows), step_rows)
            for j in range(parts):
                total = jnp.zeros((step_rows, width), F32)
                for a in range(parts):
                    total = total + u[a, at, 0:width] * coef[0, a * parts + j][None]
                    total = total + u[a, at, width:] * coef[1, a * parts + j][None]
                out_y[g, j, at, :] = (total * scale).astype(BF)
            return carry

        lax.fori_loop(0, fine // step_rows, last, 0)
        start(2, g)

    for g in range(chunks):
        wait(2, g)

    def gate(i, carry):
        at = pl.ds(pl.multiple_of(i * tile, tile), tile)
        xs = [in_y[e % chunks, e // chunks, at, :].astype(F32) for e in range(fold)]
        moved = regroup(xs, fold, width)
        for w in range(fold):
            here = pl.ds(pl.multiple_of(w * fine + i * tile, tile), tile)
            total = moved[w] + bias[...] * mixed[here, :].astype(F32)
            o_ref[here, :] = (q_feat[here, :].astype(F32) * total).astype(BF)
        return carry

    lax.fori_loop(0, fine // tile, gate, 0)

    for s in range(3):
        halo_copy(s).wait_send()
    for kind in range(3):
        for g in range(chunks):
            drain(kind, g)


def local(query, key_proj, value, short_taps, bias, long_filter):
    length, width = query.shape
    parts = lax.axis_size("ctx")
    chunks = CHUNKS
    fold = parts * chunks
    fine = length // fold
    tables = make_tables(parts, fold, length, width)
    block = pltpu.VMEM((chunks, parts, fine, width), BF)
    wide = pltpu.VMEM((parts, fine, 2 * width), BF)
    tall = pltpu.VMEM((2 * fine, 2 * width), BF)
    rows = pltpu.VMEM((length, width), BF)
    return pl.pallas_call(
        functools.partial(body, parts, fold, fine, width),
        out_shape=jax.ShapeDtypeStruct((length, width), BF),
        in_specs=[pl.BlockSpec(memory_space=pltpu.VMEM)] * 12,
        out_specs=pl.BlockSpec(memory_space=pltpu.VMEM),
        scratch_shapes=[
            pltpu.VMEM((3, 16, width), BF),
            rows, rows,
            block, block, block, block, block, block,
            wide, wide, tall, tall,
            pltpu.VMEM((chunks, parts // 2, 2 * fine, 2 * width), F32),
            pltpu.VMEM((parts, fine, 2 * width), F32),
            pltpu.SemaphoreType.DMA((3, chunks, parts)),
            pltpu.SemaphoreType.DMA((3, chunks, parts)),
            pltpu.SemaphoreType.DMA((3, chunks)),
            pltpu.SemaphoreType.DMA((3,)),
            pltpu.SemaphoreType.DMA((3,)),
        ],
        compiler_params=pltpu.CompilerParams(
            vmem_limit_bytes=56 * 1024 * 1024, collective_id=0, has_side_effects=True
        ),
    )(query, key_proj, value, short_taps, bias.reshape(1, width), long_filter, *tables)


def solution(mesh):
    in_specs = (
        P("ctx", "ch"),
        P("ctx", "ch"),
        P("ctx", "ch"),
        P(None, None, "ch"),
        P("ch"),
        P("ctx", "ch"),
    )
    return jax.shard_map(local, mesh=mesh, in_specs=in_specs, out_specs=P("ctx", "ch"), check_vma=False)
```

time: 969 us -> 88.4 us (0.09)
  the two profiles are of different devices: /device:TPU:0 before, /device:TPU:24 now
where the time goes in v2:
time: 88.4 us; the launch traced here: 88.3 us
  Pallas kernels  86 us (97%)
  local copies, waits for them, and re-layouts  2.26 us (3%)
    pallas_call x1, Pallas kernels, local(): pl.pallas_call(functools.partial(body, parts, fold, fine, width), out_sha...  86 us
    unnamed x1, local copies, waits for them, and re-layouts  2.26 us

profile of v2, /device:TPU:24, one launch (start us, length us, event | category | flops | bytes accessed | tf_op | source)
XLA Modules:
  0.0 88.3 jit_solution(12254967190221522345)
XLA Ops:
  0.0 86.0 %shard_map.118 = bf16[4096,128]{1,0:T(8,128)(2,1)} custom-call(bf16[4096,128]{1,0:T(8,128)(2,1)} %q_ref.1, bf16[4096,128]{1,0:T(8,128)(2,1)} %k_ref.1, bf16[4096,128]{1,0:T(8,128)(2,1)} %v_ref.1, f32[3,3,128]{2,1,0:T(4,128)} %taps.1, f32[1,128]{1,0:T(1,128)} %bitcast.1, bf16[4096,128]{1,0:T(8,128)(2,1)} %f_ref.1, f32[2,64,128]{2,1,0:T(8,128)} %constant.12.clone.coef, ...), custom_call_target="tpu_custom_call" | custom-call | tf_op jit(solution)/shard_map/pallas_call | solution.py:330
  86.0 2.3 %copy.14 = bf16[4096,128]{1,0:T(8,128)(2,1)} copy(bf16[4096,128]{1,0:T(8,128)(2,1)} %shard_map.118) | data formatting | bytes 2097152

commit v3 on v2

--- a/solution.py
+++ b/solution.py
@@ -11,7 +11,7 @@
 BF = jnp.bfloat16
 F32 = jnp.float32
 ROWS = 32
-CHUNKS = 2
+CHUNKS = 4
 MESH = pl.DeviceIdType.MESH
 
 
@@ -319,7 +319,7 @@
 def local(query, key_proj, value, short_taps, bias, long_filter):
     length, width = query.shape
     parts = lax.axis_size("ctx")
-    chunks = CHUNKS
+    chunks = max(1, min(CHUNKS, width // (2 * parts)))
     fold = parts * chunks
     fine = length // fold
     tables = make_tables(parts, fold, length, width)

time: 88.4 us -> 87.9 us (level)
  the two profiles are of different devices: /device:TPU:24 before, /device:TPU:0 now
where the time goes in v3:
time: 87.9 us; the launch traced here: 87.8 us
  Pallas kernels  85.5 us (97%)
  local copies, waits for them, and re-layouts  2.26 us (3%)
    pallas_call x1, Pallas kernels, local(): pl.pallas_call(functools.partial(body, parts, fold, fine, width), out_sha...  85.5 us
    unnamed x1, local copies, waits for them, and re-layouts  2.26 us

profile of v3, /device:TPU:0, one launch (start us, length us, event | category | flops | bytes accessed | tf_op | source)
XLA Modules:
  0.0 87.8 jit_solution(5791262299677562730)
XLA Ops:
  0.0 85.5 %shard_map.118 = bf16[4096,128]{1,0:T(8,128)(2,1)} custom-call(bf16[4096,128]{1,0:T(8,128)(2,1)} %q_ref.1, bf16[4096,128]{1,0:T(8,128)(2,1)} %k_ref.1, bf16[4096,128]{1,0:T(8,128)(2,1)} %v_ref.1, f32[3,3,128]{2,1,0:T(4,128)} %taps.1, f32[1,128]{1,0:T(1,128)} %bitcast.1, bf16[4096,128]{1,0:T(8,128)(2,1)} %f_ref.1, f32[2,64,128]{2,1,0:T(8,128)} %constant.12.clone.coef, ...), custom_call_target="tpu_custom_call" | custom-call | tf_op jit(solution)/shard_map/pallas_call | solution.py:330
  85.5 2.3 %copy.14 = bf16[4096,128]{1,0:T(8,128)(2,1)} copy(bf16[4096,128]{1,0:T(8,128)(2,1)} %shard_map.118) | data formatting | bytes 2097152
